TPU v7x, 512 devices: a whole 4x4x16 slice. The times are simulated.
512 devices in a mesh: dp: 16 (over z_hi, y), tensor: 32 (over z_lo, x, core).
Axes of the slice: x: 4, y: 4, z: 16 (z_hi: 4, z_lo: 4; z = z_hi * 4 + z_lo), core: 2. Of those that a mesh axis runs over, the one named last changes fastest.
Arguments:
- hidden: bfloat16 [1024, 32, 28672], P('dp', None, 'tensor'), may hold values from -6 to 6
- out_grad: bfloat16 [1024, 32, 8192], P('dp', None, 'tensor'), may hold values from -6 to 6
- proj_in: bfloat16 [28672, 64], P('tensor'), may hold values from -0.03125 to 0.03125
- proj_out: bfloat16 [8192, 64], P('tensor'), may hold values from -0.0625 to 0.0625
- lengths: int32 [1024], P('dp'), may hold values from 1 to 32, 16384 in all
- task_ids: int32 [16], replicated, may hold values from 0 to 1
Outputs:
- similarity: float32 [1024, 16, 64], P('dp', None, 'tensor')
Inputs may be any that keep to these rules, and one draw needn't show every extreme that they name: `lengths`: at least one sequence is exactly 32 long.
All inputs are finite; a program needn't handle non-finite values. No bound on the sum of `lengths` on one device may be relied on, other than what follows from the above.
Results may differ from a plain program's by a relative error of at most 0.0003.
Values sent between devices are 32-bit elements; how exact they have to be, the bound alone decides.
No kernel may reach another device: no remote copies, remote signals or barrier semaphores. Data moves between devices by JAX's collectives and lax.ppermute only.
A program may use at most 64 MiB of HBM per device.

v0:
```python
import jax
import jax.numpy as jnp
from jax import lax
from jax.sharding import PartitionSpec as P

epsilon = 1e-06


def from_behind(value, axis, steps):
    count = lax.axis_size(axis)
    pairs = [(source, (source + steps) % count) for source in range(count)]
    return lax.ppermute(value, axis, pairs)


def normalized(summed, lengths):
    seq_count, seq_len, doubled = summed.shape
    width_low = doubled // 2
    live_mask = (jnp.arange(seq_len, dtype=jnp.int32)[None, :] < lengths[:, None]).astype(
        jnp.float32
    )
    inputs_low = summed[:, :, :width_low] * live_mask[:, :, None]
    outputs_low = summed[:, :, width_low:]
    sketch = jnp.einsum("slk,slm->skm", inputs_low, outputs_low, precision=lax.Precision.HIGHEST)
    flattened = sketch.reshape(seq_count, width_low * width_low)
    root_mean = jnp.sqrt(jnp.mean(flattened * flattened, axis=1, keepdims=True) + epsilon)
    return flattened / root_mean


def inner_rows(left, right):
    return lax.dot_general(
        left,
        right,
        (((1,), (1,)), ((), ())),
        preferred_element_type=jnp.float32,
        precision=lax.Precision.HIGHEST,
    )


def body(hidden, out_grad, proj_in, proj_out, lengths, task_ids):
    block_rows, seq_len, _ = hidden.shape
    groups = lax.axis_size("dp")
    slices = lax.axis_size("tensor")
    share_rows = block_rows // slices
    group_index = lax.axis_index("dp")
    slice_index = lax.axis_index("tensor")
    width_low = proj_in.shape[1]
    factor = 1.0 / width_low
    inputs_part = jnp.dot(
        hidden.reshape(block_rows * seq_len, -1), proj_in, preferred_element_type=jnp.float32
    )
    outputs_part = jnp.dot(
        out_grad.reshape(block_rows * seq_len, -1), proj_out, preferred_element_type=jnp.float32
    )
    partial_value = jnp.concatenate([inputs_part, outputs_part], axis=1).reshape(
        block_rows, seq_len, 2 * width_low
    )
    summed = lax.psum(partial_value, "tensor")
    own_block = normalized(summed, lengths)
    mine = lax.dynamic_slice_in_dim(own_block, slice_index * share_rows, share_rows, 0)
    block_ids = jnp.arange(groups, dtype=jnp.int32)
    own_task = jnp.sum(jnp.where(block_ids == group_index, task_ids, 0))

    def place(result, visiting, source):
        source_task = jnp.sum(jnp.where(block_ids == source, task_ids, 0))
        product = inner_rows(own_block, visiting)
        piece = jnp.where(own_task == source_task, product * factor, jnp.float32(0.0))
        starts = (jnp.int32(0), source, jnp.int32(0))
        return lax.dynamic_update_slice(result, piece[:, None, :], starts)

    result = jnp.zeros((block_rows, groups, share_rows), jnp.float32)
    result = place(result, mine, group_index)

    def advance(offset, carried):
        visiting, result = carried
        visiting = from_behind(visiting, "dp", 1)
        source = (group_index - offset) % groups
        return (visiting, place(result, visiting, source))

    _, result = lax.fori_loop(1, groups, advance, (mine, result))
    return result


def solution(mesh):
    in_specs = (
        P("dp", None, "tensor"),
        P("dp", None, "tensor"),
        P("tensor", None),
        P("tensor", None),
        P("dp"),
        P(),
    )
    out_specs = P("dp", None, "tensor")
    return jax.shard_map(body, mesh=mesh, in_specs=in_specs, out_specs=out_specs, check_vma=False)
```

profile of v0, /device:TPU:128, one launch (start us, length us, event | category | flops | bytes accessed | tf_op | source)
XLA Modules:
  0.0 518.5 jit_solution(16584083541157340473)
XLA Ops:
  6.5 1.2 copy-done
  7.8 1.2 fusion.14
  8.9 3.3 fusion.13
  12.4 1.4 copy.8
  14.5 292.5 %all-reduce.2.cloned.1.call-done = f32[64,32,128]{2,1,0:T(8,128)} async-done(((f32[64,32,128]{2,1,0:T(8,128)}), f32[64,32,128]{2,1,0:T(8,128)}) %all-reduce.2.cloned.1.call-update) | async-done | bytes 1048592 | tf_op jit(solution)/shard_map/psum | solution.py:57
  307.0 6.2 %multiply_reduce_fusion = (f32[64]{0:T(128)S(1)}, f32[64,64,64]{2,1,0:T(8,128)S(1)}) fusion(f32[64,32,128]{2,1,0:T(8,128)} %all-reduce.2.cloned.1.call-done, f32[64,32]{1,0:T(8,128)S(1)} %fusion.11), kind=kOutput, calls=%fused_computation.7 | convolution fusion | flops 101318592 | bytes 3154176 | tf_op jit(solution)/shard_map/slk,slm->skm/dot_general | solution.py:23
  313.2 1.6 reshape.45
  314.9 1.4 broadcast_divide_fusion
  316.3 0.9 fusion.7
  317.2 193.9 %while.18 = (s32[]{:T(128)}, f32[2,4096]{1,0:T(2,128)S(1)}, f32[64,16,2]{0,2,1:T(2,128)S(1)}, s32[]{:T(128)}, s32[16]{0:T(128)S(1)}, /*index=5*/s32[]{:T(128)}, ...) while((s32[]{:T(128)}, f32[2,4096]{1,0:T(2,128)S(1)}, ...), condition=%wide.region_5.6_spmd.clone, body=%wide.region_3.0_spmd.clone.sunk | while | flops 6291777 | bytes 1279366 | solution.py:79
  317.2 3.4 collective-permute-start
  322.7 7.5 %collective-permute-done = f32[2,4096]{1,0:T(2,128)S(1)} collective-permute-done((f32[2,4096]{1,0:T(2,128)S(1)}, f32[2,4096]{1,0:T(2,128)S(1)}, u32[]{:S(2)}, u32[]{:S(2)}) %collective-permute-start) | collective-permute-done | bytes 32800 | tf_op jit(solution)/shard_map/while/body/eval_jaxpr/ppermute | solution.py:12
  330.2 0.9 fusion.30
  331.1 1.9 collective-permute-start
  335.1 8.0 %collective-permute-done = f32[2,4096]{1,0:T(2,128)S(1)} collective-permute-done((f32[2,4096]{1,0:T(2,128)S(1)}, f32[2,4096]{1,0:T(2,128)S(1)}, u32[]{:S(2)}, u32[]{:S(2)}) %collective-permute-start) | collective-permute-done | bytes 32800 | tf_op jit(solution)/shard_map/while/body/eval_jaxpr/ppermute | solution.py:12
  343.1 0.9 fusion.30
  344.0 1.9 collective-permute-start
  348.0 8.0 %collective-permute-done = f32[2,4096]{1,0:T(2,128)S(1)} collective-permute-done((f32[2,4096]{1,0:T(2,128)S(1)}, f32[2,4096]{1,0:T(2,128)S(1)}, u32[]{:S(2)}, u32[]{:S(2)}) %collective-permute-start) | collective-permute-done | bytes 32800 | tf_op jit(solution)/shard_map/while/body/eval_jaxpr/ppermute | solution.py:12
  356.9 1.9 collective-permute-start
  360.9 8.3 %collective-permute-done = f32[2,4096]{1,0:T(2,128)S(1)} collective-permute-done((f32[2,4096]{1,0:T(2,128)S(1)}, f32[2,4096]{1,0:T(2,128)S(1)}, u32[]{:S(2)}, u32[]{:S(2)}) %collective-permute-start) | collective-permute-done | bytes 32800 | tf_op jit(solution)/shard_map/while/body/eval_jaxpr/ppermute | solution.py:12
  370.1 1.9 collective-permute-start
  374.1 7.9 %collective-permute-done = f32[2,4096]{1,0:T(2,128)S(1)} collective-permute-done((f32[2,4096]{1,0:T(2,128)S(1)}, f32[2,4096]{1,0:T(2,128)S(1)}, u32[]{:S(2)}, u32[]{:S(2)}) %collective-permute-start) | collective-permute-done | bytes 32800 | tf_op jit(solution)/shard_map/while/body/eval_jaxpr/ppermute | solution.py:12
  382.0 0.9 fusion.30
  382.9 1.9 collective-permute-start
  386.9 7.9 %collective-permute-done = f32[2,4096]{1,0:T(2,128)S(1)} collective-permute-done((f32[2,4096]{1,0:T(2,128)S(1)}, f32[2,4096]{1,0:T(2,128)S(1)}, u32[]{:S(2)}, u32[]{:S(2)}) %collective-permute-start) | collective-permute-done | bytes 32800 | tf_op jit(solution)/shard_map/while/body/eval_jaxpr/ppermute | solution.py:12
  395.6 1.9 collective-permute-start
  399.6 8.3 %collective-permute-done = f32[2,4096]{1,0:T(2,128)S(1)} collective-permute-done((f32[2,4096]{1,0:T(2,128)S(1)}, f32[2,4096]{1,0:T(2,128)S(1)}, u32[]{:S(2)}, u32[]{:S(2)}) %collective-permute-start) | collective-permute-done | bytes 32800 | tf_op jit(solution)/shard_map/while/body/eval_jaxpr/ppermute | solution.py:12
  407.9 0.9 fusion.30
  408.8 1.9 collective-permute-start
  412.8 8.0 %collective-permute-done = f32[2,4096]{1,0:T(2,128)S(1)} collective-permute-done((f32[2,4096]{1,0:T(2,128)S(1)}, f32[2,4096]{1,0:T(2,128)S(1)}, u32[]{:S(2)}, u32[]{:S(2)}) %collective-permute-start) | collective-permute-done | bytes 32800 | tf_op jit(solution)/shard_map/while/body/eval_jaxpr/ppermute | solution.py:12
  420.7 0.9 fusion.30
  421.7 1.9 collective-permute-start
  425.6 7.9 %collective-permute-done = f32[2,4096]{1,0:T(2,128)S(1)} collective-permute-done((f32[2,4096]{1,0:T(2,128)S(1)}, f32[2,4096]{1,0:T(2,128)S(1)}, u32[]{:S(2)}, u32[]{:S(2)}) %collective-permute-start) | collective-permute-done | bytes 32800 | tf_op jit(solution)/shard_map/while/body/eval_jaxpr/ppermute | solution.py:12
  434.4 1.9 collective-permute-start
  438.4 8.0 %collective-permute-done = f32[2,4096]{1,0:T(2,128)S(1)} collective-permute-done((f32[2,4096]{1,0:T(2,128)S(1)}, f32[2,4096]{1,0:T(2,128)S(1)}, u32[]{:S(2)}, u32[]{:S(2)}) %collective-permute-start) | collective-permute-done | bytes 32800 | tf_op jit(solution)/shard_map/while/body/eval_jaxpr/ppermute | solution.py:12
  447.3 1.9 collective-permute-start
  451.3 7.9 %collective-permute-done = f32[2,4096]{1,0:T(2,128)S(1)} collective-permute-done((f32[2,4096]{1,0:T(2,128)S(1)}, f32[2,4096]{1,0:T(2,128)S(1)}, u32[]{:S(2)}, u32[]{:S(2)}) %collective-permute-start) | collective-permute-done | bytes 32800 | tf_op jit(solution)/shard_map/while/body/eval_jaxpr/ppermute | solution.py:12
  459.1 0.9 fusion.30
  460.0 1.9 collective-permute-start
  464.0 7.9 %collective-permute-done = f32[2,4096]{1,0:T(2,128)S(1)} collective-permute-done((f32[2,4096]{1,0:T(2,128)S(1)}, f32[2,4096]{1,0:T(2,128)S(1)}, u32[]{:S(2)}, u32[]{:S(2)}) %collective-permute-start) | collective-permute-done | bytes 32800 | tf_op jit(solution)/shard_map/while/body/eval_jaxpr/ppermute | solution.py:12
  471.9 0.9 fusion.30
  472.8 1.9 collective-permute-start
  476.8 7.9 %collective-permute-done = f32[2,4096]{1,0:T(2,128)S(1)} collective-permute-done((f32[2,4096]{1,0:T(2,128)S(1)}, f32[2,4096]{1,0:T(2,128)S(1)}, u32[]{:S(2)}, u32[]{:S(2)}) %collective-permute-start) | collective-permute-done | bytes 32800 | tf_op jit(solution)/shard_map/while/body/eval_jaxpr/ppermute | solution.py:12
  485.6 1.9 collective-permute-start
  489.5 7.9 %collective-permute-done = f32[2,4096]{1,0:T(2,128)S(1)} collective-permute-done((f32[2,4096]{1,0:T(2,128)S(1)}, f32[2,4096]{1,0:T(2,128)S(1)}, u32[]{:S(2)}, u32[]{:S(2)}) %collective-permute-start) | collective-permute-done | bytes 32800 | tf_op jit(solution)/shard_map/while/body/eval_jaxpr/ppermute | solution.py:12
  498.3 1.9 collective-permute-start
  502.3 7.9 %collective-permute-done = f32[2,4096]{1,0:T(2,128)S(1)} collective-permute-done((f32[2,4096]{1,0:T(2,128)S(1)}, f32[2,4096]{1,0:T(2,128)S(1)}, u32[]{:S(2)}, u32[]{:S(2)}) %collective-permute-start) | collective-permute-done | bytes 32800 | tf_op jit(solution)/shard_map/while/body/eval_jaxpr/ppermute | solution.py:12
  510.2 0.9 fusion.30
  (52 shorter events, 18.7 us)
Async XLA Ops:
  6.5 1.2 copy-start
  6.5 300.5 %all-reduce.2.cloned.1.call-start = ((), (), s32[]{:S(2)}) async-start(), calls=%async_computation | async-start | bytes 2097152 | tf_op jit(solution)/shard_map/psum | solution.py:57
  12.2 1.5 copy-start.3
  12.2 2.2 copy-start.2
  317.2 13.0 %collective-permute-start = (f32[2,4096]{1,0:T(2,128)S(1)}, f32[2,4096]{1,0:T(2,128)S(1)}, u32[]{:S(2)}, u32[]{:S(2)}) collective-permute-start(f32[2,4096]{1,0:T(2,128)S(1)} %get-tuple-element.292), channel_id=1, source_target_pairs={{0,32},{32,64},{64,96},{96,128},{128,160},{160,192},{192,224},{224... | collective-permute-start | bytes 98312 | tf_op jit(solution)/shard_map/while/body/eval_jaxpr/ppermute | solution.py:12
  331.1 12.0 %collective-permute-start = (f32[2,4096]{1,0:T(2,128)S(1)}, f32[2,4096]{1,0:T(2,128)S(1)}, u32[]{:S(2)}, u32[]{:S(2)}) collective-permute-start(f32[2,4096]{1,0:T(2,128)S(1)} %get-tuple-element.292), channel_id=1, source_target_pairs={{0,32},{32,64},{64,96},{96,128},{128,160},{160,192},{192,224},{224... | collective-permute-start | bytes 98312 | tf_op jit(solution)/shard_map/while/body/eval_jaxpr/ppermute | solution.py:12
  344.0 12.0 %collective-permute-start = (f32[2,4096]{1,0:T(2,128)S(1)}, f32[2,4096]{1,0:T(2,128)S(1)}, u32[]{:S(2)}, u32[]{:S(2)}) collective-permute-start(f32[2,4096]{1,0:T(2,128)S(1)} %get-tuple-element.292), channel_id=1, source_target_pairs={{0,32},{32,64},{64,96},{96,128},{128,160},{160,192},{192,224},{224... | collective-permute-start | bytes 98312 | tf_op jit(solution)/shard_map/while/body/eval_jaxpr/ppermute | solution.py:12
  356.9 12.2 %collective-permute-start = (f32[2,4096]{1,0:T(2,128)S(1)}, f32[2,4096]{1,0:T(2,128)S(1)}, u32[]{:S(2)}, u32[]{:S(2)}) collective-permute-start(f32[2,4096]{1,0:T(2,128)S(1)} %get-tuple-element.292), channel_id=1, source_target_pairs={{0,32},{32,64},{64,96},{96,128},{128,160},{160,192},{192,224},{224... | collective-permute-start | bytes 98312 | tf_op jit(solution)/shard_map/while/body/eval_jaxpr/ppermute | solution.py:12
  370.1 11.9 %collective-permute-start = (f32[2,4096]{1,0:T(2,128)S(1)}, f32[2,4096]{1,0:T(2,128)S(1)}, u32[]{:S(2)}, u32[]{:S(2)}) collective-permute-start(f32[2,4096]{1,0:T(2,128)S(1)} %get-tuple-element.292), channel_id=1, source_target_pairs={{0,32},{32,64},{64,96},{96,128},{128,160},{160,192},{192,224},{224... | collective-permute-start | bytes 98312 | tf_op jit(solution)/shard_map/while/body/eval_jaxpr/ppermute | solution.py:12
  382.9 11.8 %collective-permute-start = (f32[2,4096]{1,0:T(2,128)S(1)}, f32[2,4096]{1,0:T(2,128)S(1)}, u32[]{:S(2)}, u32[]{:S(2)}) collective-permute-start(f32[2,4096]{1,0:T(2,128)S(1)} %get-tuple-element.292), channel_id=1, source_target_pairs={{0,32},{32,64},{64,96},{96,128},{128,160},{160,192},{192,224},{224... | collective-permute-start | bytes 98312 | tf_op jit(solution)/shard_map/while/body/eval_jaxpr/ppermute | solution.py:12
  395.6 12.2 %collective-permute-start = (f32[2,4096]{1,0:T(2,128)S(1)}, f32[2,4096]{1,0:T(2,128)S(1)}, u32[]{:S(2)}, u32[]{:S(2)}) collective-permute-start(f32[2,4096]{1,0:T(2,128)S(1)} %get-tuple-element.292), channel_id=1, source_target_pairs={{0,32},{32,64},{64,96},{96,128},{128,160},{160,192},{192,224},{224... | collective-permute-start | bytes 98312 | tf_op jit(solution)/shard_map/while/body/eval_jaxpr/ppermute | solution.py:12
  408.8 11.9 %collective-permute-start = (f32[2,4096]{1,0:T(2,128)S(1)}, f32[2,4096]{1,0:T(2,128)S(1)}, u32[]{:S(2)}, u32[]{:S(2)}) collective-permute-start(f32[2,4096]{1,0:T(2,128)S(1)} %get-tuple-element.292), channel_id=1, source_target_pairs={{0,32},{32,64},{64,96},{96,128},{128,160},{160,192},{192,224},{224... | collective-permute-start | bytes 98312 | tf_op jit(solution)/shard_map/while/body/eval_jaxpr/ppermute | solution.py:12
  421.7 11.9 %collective-permute-start = (f32[2,4096]{1,0:T(2,128)S(1)}, f32[2,4096]{1,0:T(2,128)S(1)}, u32[]{:S(2)}, u32[]{:S(2)}) collective-permute-start(f32[2,4096]{1,0:T(2,128)S(1)} %get-tuple-element.292), channel_id=1, source_target_pairs={{0,32},{32,64},{64,96},{96,128},{128,160},{160,192},{192,224},{224... | collective-permute-start | bytes 98312 | tf_op jit(solution)/shard_map/while/body/eval_jaxpr/ppermute | solution.py:12
  434.4 11.9 %collective-permute-start = (f32[2,4096]{1,0:T(2,128)S(1)}, f32[2,4096]{1,0:T(2,128)S(1)}, u32[]{:S(2)}, u32[]{:S(2)}) collective-permute-start(f32[2,4096]{1,0:T(2,128)S(1)} %get-tuple-element.292), channel_id=1, source_target_pairs={{0,32},{32,64},{64,96},{96,128},{128,160},{160,192},{192,224},{224... | collective-permute-start | bytes 98312 | tf_op jit(solution)/shard_map/while/body/eval_jaxpr/ppermute | solution.py:12
  447.3 11.8 %collective-permute-start = (f32[2,4096]{1,0:T(2,128)S(1)}, f32[2,4096]{1,0:T(2,128)S(1)}, u32[]{:S(2)}, u32[]{:S(2)}) collective-permute-start(f32[2,4096]{1,0:T(2,128)S(1)} %get-tuple-element.292), channel_id=1, source_target_pairs={{0,32},{32,64},{64,96},{96,128},{128,160},{160,192},{192,224},{224... | collective-permute-start | bytes 98312 | tf_op jit(solution)/shard_map/while/body/eval_jaxpr/ppermute | solution.py:12
  460.0 11.8 %collective-permute-start = (f32[2,4096]{1,0:T(2,128)S(1)}, f32[2,4096]{1,0:T(2,128)S(1)}, u32[]{:S(2)}, u32[]{:S(2)}) collective-permute-start(f32[2,4096]{1,0:T(2,128)S(1)} %get-tuple-element.292), channel_id=1, source_target_pairs={{0,32},{32,64},{64,96},{96,128},{128,160},{160,192},{192,224},{224... | collective-permute-start | bytes 98312 | tf_op jit(solution)/shard_map/while/body/eval_jaxpr/ppermute | solution.py:12
  472.8 11.8 %collective-permute-start = (f32[2,4096]{1,0:T(2,128)S(1)}, f32[2,4096]{1,0:T(2,128)S(1)}, u32[]{:S(2)}, u32[]{:S(2)}) collective-permute-start(f32[2,4096]{1,0:T(2,128)S(1)} %get-tuple-element.292), channel_id=1, source_target_pairs={{0,32},{32,64},{64,96},{96,128},{128,160},{160,192},{192,224},{224... | collective-permute-start | bytes 98312 | tf_op jit(solution)/shard_map/while/body/eval_jaxpr/ppermute | solution.py:12
  485.6 11.8 %collective-permute-start = (f32[2,4096]{1,0:T(2,128)S(1)}, f32[2,4096]{1,0:T(2,128)S(1)}, u32[]{:S(2)}, u32[]{:S(2)}) collective-permute-start(f32[2,4096]{1,0:T(2,128)S(1)} %get-tuple-element.292), channel_id=1, source_target_pairs={{0,32},{32,64},{64,96},{96,128},{128,160},{160,192},{192,224},{224... | collective-permute-start | bytes 98312 | tf_op jit(solution)/shard_map/while/body/eval_jaxpr/ppermute | solution.py:12
  498.3 11.8 %collective-permute-start = (f32[2,4096]{1,0:T(2,128)S(1)}, f32[2,4096]{1,0:T(2,128)S(1)}, u32[]{:S(2)}, u32[]{:S(2)}) collective-permute-start(f32[2,4096]{1,0:T(2,128)S(1)} %get-tuple-element.292), channel_id=1, source_target_pairs={{0,32},{32,64},{64,96},{96,128},{128,160},{160,192},{192,224},{224... | collective-permute-start | bytes 98312 | tf_op jit(solution)/shard_map/while/body/eval_jaxpr/ppermute | solution.py:12
  511.1 0.6 copy-start.1
Sparse Core Ops, SparseCore 0:
  13.9 293.0 all-reduce.1
where the time goes:
time: 519 us
  waiting for transfers between devices  411 us (79%)
  starting transfers between devices  30.3 us (6%)
  matrix products  25.5 us (5%)
  loops' own time  20 us (4%)
  between operations  13.5 us (3%)
  other arithmetic  12.9 us (2%)
    psum x1, waiting for transfers between devices, body(): summed = lax.psum(partial_value, 'tensor')  292 us
    ppermute x15, waiting for transfers between devices, from_behind(): return lax.ppermute(value, axis, pairs)  119 us
    ppermute x15, starting transfers between devices, from_behind(): return lax.ppermute(value, axis, pairs)  30.3 us
    another operation x1, loops' own time, body(): _, result = lax.fori_loop(1, groups, advance, (mine, result))  20 us
    dot_general x16, matrix products, inner_rows(): lax.dot_general(left, right, (((1,), (1,)), ((), ())), preferred_element_...  14.8 us
    reduce_sum x15, other arithmetic, place(): source_task = jnp.sum(jnp.where(block_ids == source, task_ids, 0))  10.7 us
  transfers between devices with their start and end apart: 16, of which 16 were waited for; matrix products, arithmetic and copies ran while one was open for 2% of the time, Pallas kernels for 0%

commit v1 on v0

--- a/solution.py
+++ b/solution.py
@@ -54,7 +54,8 @@
     partial_value = jnp.concatenate([inputs_part, outputs_part], axis=1).reshape(
         block_rows, seq_len, 2 * width_low
     )
-    summed = lax.psum(partial_value, "tensor")
+    parts = lax.all_gather(partial_value, "tensor")
+    summed = jnp.sum(parts, axis=0)
     own_block = normalized(summed, lengths)
     mine = lax.dynamic_slice_in_dim(own_block, slice_index * share_rows, share_rows, 0)
     block_ids = jnp.arange(groups, dtype=jnp.int32)

time: 519 us -> 431 us (0.83)
  the two profiles are of different devices: /device:TPU:128 before, /device:TPU:226 now
where the time goes in v1:
time: 431 us
  waiting for transfers between devices  313 us (73%)
  starting transfers between devices  30.3 us (7%)
  matrix products  25.2 us (6%)
  other arithmetic  23.9 us (6%)
  loops' own time  19.5 us (5%)
  between operations  13.5 us (3%)
  local copies, waits for them, and re-layouts  5.38 us (1%)
    all_gather x1, waiting for transfers between devices, body(): parts = lax.all_gather(partial_value, 'tensor')  191 us
    ppermute x15, waiting for transfers between devices, from_behind(): return lax.ppermute(value, axis, pairs)  122 us
    ppermute x15, starting transfers between devices, from_behind(): return lax.ppermute(value, axis, pairs)  30.3 us
    another operation x1, loops' own time, body(): _, result = lax.fori_loop(1, groups, advance, (mine, result))  19.5 us
    dot_general x16, matrix products, inner_rows(): lax.dot_general(left, right, (((1,), (1,)), ((), ())), preferred_element_...  14.8 us
    reduce_sum x1, other arithmetic, body(): summed = jnp.sum(parts, axis=0)  12.3 us
    reduce_sum x15, other arithmetic, place(): source_task = jnp.sum(jnp.where(block_ids == source, task_ids, 0))  10.7 us
  transfers between devices with their start and end apart: 16, of which 16 were waited for; matrix products, arithmetic and copies ran while one was open for 3% of the time, Pallas kernels for 0%

profile of v1, /device:TPU:226, one launch (start us, length us, event | category | flops | bytes accessed | tf_op | source)
XLA Modules:
  0.0 430.5 jit_solution(7104620938526733610)
XLA Ops:
  6.5 1.2 copy-done
  7.8 1.2 fusion.14
  8.9 3.3 fusion.13
  12.4 1.3 copy.8
  14.4 190.5 %all-gather.2.cloned.1.call-done = f32[32,64,32,128]{3,2,1,0:T(8,128)} async-done(((f32[1,64,32,128]{3,2,1,0:T(8,128)}), f32[32,64,32,128]{3,2,1,0:T(8,128)}) %all-gather.2.cloned.1.call-update) | async-done | bytes 33554448 | tf_op jit(solution)/shard_map/all_gather | solution.py:57
  204.9 12.3 %reduce_sum.47 = f32[64,32,128]{2,1,0:T(8,128)S(1)} reduce(f32[32,64,32,128]{3,2,1,0:T(8,128)} %all-gather.2.cloned.1.call-done, f32[]{:T(128)} %constant.84.clone.1), dimensions={0}, to_apply=%region_0.0 | reduce | flops 8126464 | bytes 34603012 | tf_op jit(solution)/shard_map/reduce_sum | solution.py:58
  217.2 5.9 %multiply_reduce_fusion = (f32[64]{0:T(128)S(1)}, f32[64,64,64]{2,1,0:T(8,128)}) fusion(f32[64,32,128]{2,1,0:T(8,128)S(1)} %reduce_sum.47, f32[64,32]{1,0:T(8,128)S(1)} %fusion.11), kind=kOutput, calls=%fused_computation.7 | convolution fusion | flops 101318592 | bytes 3178752 | tf_op jit(solution)/shard_map/slk,slm->skm/dot_general | solution.py:23
  223.1 2.1 reshape.41
  225.5 0.9 fusion.7
  226.4 196.6 %while.18 = (s32[]{:T(128)}, f32[2,4096]{1,0:T(2,128)S(1)}, f32[64,16,2]{0,2,1:T(2,128)S(1)}, s32[]{:T(128)}, s32[16]{0:T(128)S(1)}, /*index=5*/s32[]{:T(128)}, ...) while((s32[]{:T(128)}, f32[2,4096]{1,0:T(2,128)S(1)}, ...), condition=%wide.region_5.6_spmd.clone, body=%wide.region_3.0_spmd.clone.sunk | while | flops 6291777 | bytes 1279366 | solution.py:80
  226.4 3.4 collective-permute-start
  231.8 7.9 %collective-permute-done = f32[2,4096]{1,0:T(2,128)S(1)} collective-permute-done((f32[2,4096]{1,0:T(2,128)S(1)}, f32[2,4096]{1,0:T(2,128)S(1)}, u32[]{:S(2)}, u32[]{:S(2)}) %collective-permute-start) | collective-permute-done | bytes 32800 | tf_op jit(solution)/shard_map/while/body/eval_jaxpr/ppermute | solution.py:12
  239.7 0.9 fusion.30
  240.6 1.9 collective-permute-start
  244.6 8.7 %collective-permute-done = f32[2,4096]{1,0:T(2,128)S(1)} collective-permute-done((f32[2,4096]{1,0:T(2,128)S(1)}, f32[2,4096]{1,0:T(2,128)S(1)}, u32[]{:S(2)}, u32[]{:S(2)}) %collective-permute-start) | collective-permute-done | bytes 32800 | tf_op jit(solution)/shard_map/while/body/eval_jaxpr/ppermute | solution.py:12
  253.3 0.9 fusion.30
  254.2 1.9 collective-permute-start
  258.1 8.3 %collective-permute-done = f32[2,4096]{1,0:T(2,128)S(1)} collective-permute-done((f32[2,4096]{1,0:T(2,128)S(1)}, f32[2,4096]{1,0:T(2,128)S(1)}, u32[]{:S(2)}, u32[]{:S(2)}) %collective-permute-start) | collective-permute-done | bytes 32800 | tf_op jit(solution)/shard_map/while/body/eval_jaxpr/ppermute | solution.py:12
  266.4 0.9 fusion.30
  267.4 1.9 collective-permute-start
  271.3 8.0 %collective-permute-done = f32[2,4096]{1,0:T(2,128)S(1)} collective-permute-done((f32[2,4096]{1,0:T(2,128)S(1)}, f32[2,4096]{1,0:T(2,128)S(1)}, u32[]{:S(2)}, u32[]{:S(2)}) %collective-permute-start) | collective-permute-done | bytes 32800 | tf_op jit(solution)/shard_map/while/body/eval_jaxpr/ppermute | solution.py:12
  279.3 0.9 fusion.30
  280.2 1.9 collective-permute-start
  284.1 7.9 %collective-permute-done = f32[2,4096]{1,0:T(2,128)S(1)} collective-permute-done((f32[2,4096]{1,0:T(2,128)S(1)}, f32[2,4096]{1,0:T(2,128)S(1)}, u32[]{:S(2)}, u32[]{:S(2)}) %collective-permute-start) | collective-permute-done | bytes 32800 | tf_op jit(solution)/shard_map/while/body/eval_jaxpr/ppermute | solution.py:12
  293.0 1.9 collective-permute-start
  296.9 7.9 %collective-permute-done = f32[2,4096]{1,0:T(2,128)S(1)} collective-permute-done((f32[2,4096]{1,0:T(2,128)S(1)}, f32[2,4096]{1,0:T(2,128)S(1)}, u32[]{:S(2)}, u32[]{:S(2)}) %collective-permute-start) | collective-permute-done | bytes 32800 | tf_op jit(solution)/shard_map/while/body/eval_jaxpr/ppermute | solution.py:12
  305.7 1.9 collective-permute-start
  309.7 8.0 %collective-permute-done = f32[2,4096]{1,0:T(2,128)S(1)} collective-permute-done((f32[2,4096]{1,0:T(2,128)S(1)}, f32[2,4096]{1,0:T(2,128)S(1)}, u32[]{:S(2)}, u32[]{:S(2)}) %collective-permute-start) | collective-permute-done | bytes 32800 | tf_op jit(solution)/shard_map/while/body/eval_jaxpr/ppermute | solution.py:12
  317.6 0.9 fusion.30
  318.6 1.9 collective-permute-start
  322.5 7.9 %collective-permute-done = f32[2,4096]{1,0:T(2,128)S(1)} collective-permute-done((f32[2,4096]{1,0:T(2,128)S(1)}, f32[2,4096]{1,0:T(2,128)S(1)}, u32[]{:S(2)}, u32[]{:S(2)}) %collective-permute-start) | collective-permute-done | bytes 32800 | tf_op jit(solution)/shard_map/while/body/eval_jaxpr/ppermute | solution.py:12
  331.3 1.9 collective-permute-start
  335.3 8.1 %collective-permute-done = f32[2,4096]{1,0:T(2,128)S(1)} collective-permute-done((f32[2,4096]{1,0:T(2,128)S(1)}, f32[2,4096]{1,0:T(2,128)S(1)}, u32[]{:S(2)}, u32[]{:S(2)}) %collective-permute-start) | collective-permute-done | bytes 32800 | tf_op jit(solution)/shard_map/while/body/eval_jaxpr/ppermute | solution.py:12
  344.3 1.9 collective-permute-start
  348.2 9.2 %collective-permute-done = f32[2,4096]{1,0:T(2,128)S(1)} collective-permute-done((f32[2,4096]{1,0:T(2,128)S(1)}, f32[2,4096]{1,0:T(2,128)S(1)}, u32[]{:S(2)}, u32[]{:S(2)}) %collective-permute-start) | collective-permute-done | bytes 32800 | tf_op jit(solution)/shard_map/while/body/eval_jaxpr/ppermute | solution.py:12
  357.4 0.9 fusion.30
  358.4 1.9 collective-permute-start
  362.3 8.4 %collective-permute-done = f32[2,4096]{1,0:T(2,128)S(1)} collective-permute-done((f32[2,4096]{1,0:T(2,128)S(1)}, f32[2,4096]{1,0:T(2,128)S(1)}, u32[]{:S(2)}, u32[]{:S(2)}) %collective-permute-start) | collective-permute-done | bytes 32800 | tf_op jit(solution)/shard_map/while/body/eval_jaxpr/ppermute | solution.py:12
  371.6 1.9 collective-permute-start
  375.6 8.3 %collective-permute-done = f32[2,4096]{1,0:T(2,128)S(1)} collective-permute-done((f32[2,4096]{1,0:T(2,128)S(1)}, f32[2,4096]{1,0:T(2,128)S(1)}, u32[]{:S(2)}, u32[]{:S(2)}) %collective-permute-start) | collective-permute-done | bytes 32800 | tf_op jit(solution)/shard_map/while/body/eval_jaxpr/ppermute | solution.py:12
  383.9 0.9 fusion.30
  384.8 1.9 collective-permute-start
  388.7 7.9 %collective-permute-done = f32[2,4096]{1,0:T(2,128)S(1)} collective-permute-done((f32[2,4096]{1,0:T(2,128)S(1)}, f32[2,4096]{1,0:T(2,128)S(1)}, u32[]{:S(2)}, u32[]{:S(2)}) %collective-permute-start) | collective-permute-done | bytes 32800 | tf_op jit(solution)/shard_map/while/body/eval_jaxpr/ppermute | solution.py:12
  396.6 0.9 fusion.30
  397.5 1.9 collective-permute-start
  401.5 7.9 %collective-permute-done = f32[2,4096]{1,0:T(2,128)S(1)} collective-permute-done((f32[2,4096]{1,0:T(2,128)S(1)}, f32[2,4096]{1,0:T(2,128)S(1)}, u32[]{:S(2)}, u32[]{:S(2)}) %collective-permute-start) | collective-permute-done | bytes 32800 | tf_op jit(solution)/shard_map/while/body/eval_jaxpr/ppermute | solution.py:12
  410.3 1.9 collective-permute-start
  414.2 7.9 %collective-permute-done = f32[2,4096]{1,0:T(2,128)S(1)} collective-permute-done((f32[2,4096]{1,0:T(2,128)S(1)}, f32[2,4096]{1,0:T(2,128)S(1)}, u32[]{:S(2)}, u32[]{:S(2)}) %collective-permute-start) | collective-permute-done | bytes 32800 | tf_op jit(solution)/shard_map/while/body/eval_jaxpr/ppermute | solution.py:12
  (53 shorter events, 18.8 us)
Async XLA Ops:
  6.5 1.2 copy-start
  6.5 198.4 %all-gather.2.cloned.1.call-start = ((), (), s32[]{:S(2)}) async-start(), calls=%async_computation | async-start | bytes 34603008 | tf_op jit(solution)/shard_map/all_gather | solution.py:57
  12.2 1.5 copy-start.3
  12.2 2.1 copy-start.2
  226.4 13.3 %collective-permute-start = (f32[2,4096]{1,0:T(2,128)S(1)}, f32[2,4096]{1,0:T(2,128)S(1)}, u32[]{:S(2)}, u32[]{:S(2)}) collective-permute-start(f32[2,4096]{1,0:T(2,128)S(1)} %get-tuple-element.292), channel_id=1, source_target_pairs={{0,32},{32,64},{64,96},{96,128},{128,160},{160,192},{192,224},{224... | collective-permute-start | bytes 98312 | tf_op jit(solution)/shard_map/while/body/eval_jaxpr/ppermute | solution.py:12
  240.6 12.6 %collective-permute-start = (f32[2,4096]{1,0:T(2,128)S(1)}, f32[2,4096]{1,0:T(2,128)S(1)}, u32[]{:S(2)}, u32[]{:S(2)}) collective-permute-start(f32[2,4096]{1,0:T(2,128)S(1)} %get-tuple-element.292), channel_id=1, source_target_pairs={{0,32},{32,64},{64,96},{96,128},{128,160},{160,192},{192,224},{224... | collective-permute-start | bytes 98312 | tf_op jit(solution)/shard_map/while/body/eval_jaxpr/ppermute | solution.py:12
  254.2 12.3 %collective-permute-start = (f32[2,4096]{1,0:T(2,128)S(1)}, f32[2,4096]{1,0:T(2,128)S(1)}, u32[]{:S(2)}, u32[]{:S(2)}) collective-permute-start(f32[2,4096]{1,0:T(2,128)S(1)} %get-tuple-element.292), channel_id=1, source_target_pairs={{0,32},{32,64},{64,96},{96,128},{128,160},{160,192},{192,224},{224... | collective-permute-start | bytes 98312 | tf_op jit(solution)/shard_map/while/body/eval_jaxpr/ppermute | solution.py:12
  267.4 11.9 %collective-permute-start = (f32[2,4096]{1,0:T(2,128)S(1)}, f32[2,4096]{1,0:T(2,128)S(1)}, u32[]{:S(2)}, u32[]{:S(2)}) collective-permute-start(f32[2,4096]{1,0:T(2,128)S(1)} %get-tuple-element.292), channel_id=1, source_target_pairs={{0,32},{32,64},{64,96},{96,128},{128,160},{160,192},{192,224},{224... | collective-permute-start | bytes 98312 | tf_op jit(solution)/shard_map/while/body/eval_jaxpr/ppermute | solution.py:12
  280.2 11.9 %collective-permute-start = (f32[2,4096]{1,0:T(2,128)S(1)}, f32[2,4096]{1,0:T(2,128)S(1)}, u32[]{:S(2)}, u32[]{:S(2)}) collective-permute-start(f32[2,4096]{1,0:T(2,128)S(1)} %get-tuple-element.292), channel_id=1, source_target_pairs={{0,32},{32,64},{64,96},{96,128},{128,160},{160,192},{192,224},{224... | collective-permute-start | bytes 98312 | tf_op jit(solution)/shard_map/while/body/eval_jaxpr/ppermute | solution.py:12
  293.0 11.8 %collective-permute-start = (f32[2,4096]{1,0:T(2,128)S(1)}, f32[2,4096]{1,0:T(2,128)S(1)}, u32[]{:S(2)}, u32[]{:S(2)}) collective-permute-start(f32[2,4096]{1,0:T(2,128)S(1)} %get-tuple-element.292), channel_id=1, source_target_pairs={{0,32},{32,64},{64,96},{96,128},{128,160},{160,192},{192,224},{224... | collective-permute-start | bytes 98312 | tf_op jit(solution)/shard_map/while/body/eval_jaxpr/ppermute | solution.py:12
  305.7 11.9 %collective-permute-start = (f32[2,4096]{1,0:T(2,128)S(1)}, f32[2,4096]{1,0:T(2,128)S(1)}, u32[]{:S(2)}, u32[]{:S(2)}) collective-permute-start(f32[2,4096]{1,0:T(2,128)S(1)} %get-tuple-element.292), channel_id=1, source_target_pairs={{0,32},{32,64},{64,96},{96,128},{128,160},{160,192},{192,224},{224... | collective-permute-start | bytes 98312 | tf_op jit(solution)/shard_map/while/body/eval_jaxpr/ppermute | solution.py:12
  318.6 11.9 %collective-permute-start = (f32[2,4096]{1,0:T(2,128)S(1)}, f32[2,4096]{1,0:T(2,128)S(1)}, u32[]{:S(2)}, u32[]{:S(2)}) collective-permute-start(f32[2,4096]{1,0:T(2,128)S(1)} %get-tuple-element.292), channel_id=1, source_target_pairs={{0,32},{32,64},{64,96},{96,128},{128,160},{160,192},{192,224},{224... | collective-permute-start | bytes 98312 | tf_op jit(solution)/shard_map/while/body/eval_jaxpr/ppermute | solution.py:12
  331.3 12.0 %collective-permute-start = (f32[2,4096]{1,0:T(2,128)S(1)}, f32[2,4096]{1,0:T(2,128)S(1)}, u32[]{:S(2)}, u32[]{:S(2)}) collective-permute-start(f32[2,4096]{1,0:T(2,128)S(1)} %get-tuple-element.292), channel_id=1, source_target_pairs={{0,32},{32,64},{64,96},{96,128},{128,160},{160,192},{192,224},{224... | collective-permute-start | bytes 98312 | tf_op jit(solution)/shard_map/while/body/eval_jaxpr/ppermute | solution.py:12
  344.3 13.1 %collective-permute-start = (f32[2,4096]{1,0:T(2,128)S(1)}, f32[2,4096]{1,0:T(2,128)S(1)}, u32[]{:S(2)}, u32[]{:S(2)}) collective-permute-start(f32[2,4096]{1,0:T(2,128)S(1)} %get-tuple-element.292), channel_id=1, source_target_pairs={{0,32},{32,64},{64,96},{96,128},{128,160},{160,192},{192,224},{224... | collective-permute-start | bytes 98312 | tf_op jit(solution)/shard_map/while/body/eval_jaxpr/ppermute | solution.py:12
  358.4 12.4 %collective-permute-start = (f32[2,4096]{1,0:T(2,128)S(1)}, f32[2,4096]{1,0:T(2,128)S(1)}, u32[]{:S(2)}, u32[]{:S(2)}) collective-permute-start(f32[2,4096]{1,0:T(2,128)S(1)} %get-tuple-element.292), channel_id=1, source_target_pairs={{0,32},{32,64},{64,96},{96,128},{128,160},{160,192},{192,224},{224... | collective-permute-start | bytes 98312 | tf_op jit(solution)/shard_map/while/body/eval_jaxpr/ppermute | solution.py:12
  371.6 12.2 %collective-permute-start = (f32[2,4096]{1,0:T(2,128)S(1)}, f32[2,4096]{1,0:T(2,128)S(1)}, u32[]{:S(2)}, u32[]{:S(2)}) collective-permute-start(f32[2,4096]{1,0:T(2,128)S(1)} %get-tuple-element.292), channel_id=1, source_target_pairs={{0,32},{32,64},{64,96},{96,128},{128,160},{160,192},{192,224},{224... | collective-permute-start | bytes 98312 | tf_op jit(solution)/shard_map/while/body/eval_jaxpr/ppermute | solution.py:12
  384.8 11.8 %collective-permute-start = (f32[2,4096]{1,0:T(2,128)S(1)}, f32[2,4096]{1,0:T(2,128)S(1)}, u32[]{:S(2)}, u32[]{:S(2)}) collective-permute-start(f32[2,4096]{1,0:T(2,128)S(1)} %get-tuple-element.292), channel_id=1, source_target_pairs={{0,32},{32,64},{64,96},{96,128},{128,160},{160,192},{192,224},{224... | collective-permute-start | bytes 98312 | tf_op jit(solution)/shard_map/while/body/eval_jaxpr/ppermute | solution.py:12
  397.5 11.8 %collective-permute-start = (f32[2,4096]{1,0:T(2,128)S(1)}, f32[2,4096]{1,0:T(2,128)S(1)}, u32[]{:S(2)}, u32[]{:S(2)}) collective-permute-start(f32[2,4096]{1,0:T(2,128)S(1)} %get-tuple-element.292), channel_id=1, source_target_pairs={{0,32},{32,64},{64,96},{96,128},{128,160},{160,192},{192,224},{224... | collective-permute-start | bytes 98312 | tf_op jit(solution)/shard_map/while/body/eval_jaxpr/ppermute | solution.py:12
  410.3 11.8 %collective-permute-start = (f32[2,4096]{1,0:T(2,128)S(1)}, f32[2,4096]{1,0:T(2,128)S(1)}, u32[]{:S(2)}, u32[]{:S(2)}) collective-permute-start(f32[2,4096]{1,0:T(2,128)S(1)} %get-tuple-element.292), channel_id=1, source_target_pairs={{0,32},{32,64},{64,96},{96,128},{128,160},{160,192},{192,224},{224... | collective-permute-start | bytes 98312 | tf_op jit(solution)/shard_map/while/body/eval_jaxpr/ppermute | solution.py:12
  423.0 0.6 copy-start.1
Sparse Core Ops, SparseCore 0:
  13.8 191.0 all-gather.1
